TPU v7x, 32 devices: a whole 2x2x4 slice. The times are simulated.
32 devices in a mesh: tensor: 4 (over x, core), section: 2 (over y), dp: 4 (over z).
Axes of the slice: x: 2, y: 2, z: 4, core: 2. Of those that a mesh axis runs over, the one named last changes fastest.
Arguments:
- block_input: bfloat16 [4096, 6144], P(('section', 'dp')), may hold values from -6 to 6
- output_gradient: bfloat16 [4096, 6144], P(('section', 'dp')), may hold values from -6 to 6
- queries: bfloat16 [4096, 3072], P(('section', 'dp'), 'tensor'), may hold values from -8 to 8
- saved_keys: bfloat16 [4096, 3072], P(('section', 'dp'), 'tensor'), may hold values from -8 to 8
- values: bfloat16 [4096, 3072], P(('section', 'dp'), 'tensor'), may hold values from -6 to 6
- document_index: int32 [4096], P(('section', 'dp')), may hold values from 0 to 4095, as said below
- output_weight: bfloat16 [6144, 3072], P(('section', 'dp'), 'tensor'), may hold values from -0.109375 to 0.109375
- adapter_down_weight: bfloat16 [2, 6144, 128], P('section'), may hold values from -0.078125 to 0.078125
- adapter_up_weight: bfloat16 [2, 128, 3072], P('section', None, 'tensor'), may hold values from -0.5 to 0.5
Outputs:
- grad_out: float32 [6144, 3072], P(('section', 'dp'), 'tensor')
- grad_value_proj: float32 [6144, 3072], P(('section', 'dp'), 'tensor')
- grad_query: bfloat16 [4096, 3072], P(('section', 'dp'), 'tensor')
- grad_key: bfloat16 [4096, 3072], P(('section', 'dp'), 'tensor')
- grad_down: float32 [2, 6144, 128], P('section', 'dp')
- grad_up: float32 [2, 128, 3072], P('section', 'dp', 'tensor')
Inputs may be any that keep to these rules, and one draw needn't show every extreme that they name: `document_index`: ids never fall along the tokens; a document's id is the index of its first token, each block of 512 tokens starts a new document, and the last token is a document of its own.
All inputs are finite; a program needn't handle non-finite values.
Results may differ from a plain program's by a relative error of at most 0.015.
Values may be sent and summed in bfloat16 or wider, within the bound.
A program may use at most 192 MiB of HBM per device.

v0:
```python
import jax
import jax.numpy as jnp
from jax import lax
from jax.sharding import PartitionSpec as P

HD = 128


def attend(queries, saved_keys, values, attn_grad, document_index):
    token_rows = queries.shape[0]
    head_count = queries.shape[1] // HD
    score_scale = HD ** (-0.5)
    query_heads = queries.reshape(token_rows, head_count, HD)
    key_heads = saved_keys.reshape(token_rows, head_count, HD)
    value_heads = values.reshape(token_rows, head_count, HD)
    grad_heads = attn_grad.reshape(token_rows, head_count, HD)
    scores = (
        jnp.einsum("qhd,khd->hqk", query_heads, key_heads, preferred_element_type=jnp.float32)
        * score_scale
    )
    position = jnp.arange(token_rows, dtype=jnp.int32)
    allowed = (document_index[:, None] == document_index[None, :]) & (
        position[None, :] <= position[:, None]
    )
    scores = jnp.where(allowed[None], scores, jnp.float32(-1e30))
    top_score = jnp.max(scores, axis=-1, keepdims=True)
    expo = jnp.exp(scores - top_score)
    attn_probs = expo / jnp.sum(expo, axis=-1, keepdims=True)
    probs_half = attn_probs.astype(jnp.bfloat16)
    output = jnp.einsum(
        "hqk,khd->qhd", probs_half, value_heads, preferred_element_type=jnp.float32
    ).astype(jnp.bfloat16)
    value_gradient = jnp.einsum(
        "hqk,qhd->khd", probs_half, grad_heads, preferred_element_type=jnp.float32
    ).astype(jnp.bfloat16)
    grad_prob = jnp.einsum(
        "qhd,khd->hqk", grad_heads, value_heads, preferred_element_type=jnp.float32
    )
    row_delta = jnp.sum(attn_probs * grad_prob, axis=-1, keepdims=True)
    grad_score = (attn_probs * (grad_prob - row_delta) * score_scale).astype(jnp.bfloat16)
    grad_query = jnp.einsum(
        "hqk,khd->qhd", grad_score, key_heads, preferred_element_type=jnp.float32
    ).astype(jnp.bfloat16)
    grad_key = jnp.einsum(
        "hqk,qhd->khd", grad_score, query_heads, preferred_element_type=jnp.float32
    ).astype(jnp.bfloat16)
    width = head_count * HD
    return (
        output.reshape(token_rows, width),
        value_gradient.reshape(token_rows, width),
        grad_query.reshape(token_rows, width),
        grad_key.reshape(token_rows, width),
    )


def local(
    block_input,
    output_gradient,
    queries,
    saved_keys,
    values,
    document_index,
    output_weight,
    adapter_down_weight,
    adapter_up_weight,
):
    token_rows = block_input.shape[0]
    local_width = queries.shape[1]
    contract_rows = (((0,), (0,)), ((), ()))
    grad_cols = output_gradient
    attn_grad = jnp.dot(
        grad_cols,
        lax.all_gather(output_weight, ("section", "dp"), axis=0, tiled=True),
        preferred_element_type=jnp.float32,
    ).astype(jnp.bfloat16)
    output, value_gradient, grad_query, grad_key = attend(
        queries, saved_keys, values, attn_grad, document_index
    )
    grad_cols = output_gradient
    out_term = lax.dot_general(grad_cols, output, contract_rows, preferred_element_type=jnp.float32)
    value_term = lax.dot_general(
        block_input, value_gradient, contract_rows, preferred_element_type=jnp.float32
    )
    summed = lax.psum_scatter(
        jnp.concatenate([out_term, value_term], axis=1).astype(jnp.bfloat16),
        ("section", "dp"),
        scatter_dimension=0,
        tiled=True,
    ).astype(jnp.float32)
    narrow_product = jnp.dot(
        block_input, adapter_down_weight[0], preferred_element_type=jnp.float32
    ).astype(jnp.bfloat16)
    mix_part = lax.dot_general(
        value_gradient,
        adapter_up_weight[0],
        (((1,), (1,)), ((), ())),
        preferred_element_type=jnp.float32,
    )
    mix_term = lax.psum(mix_part.astype(jnp.bfloat16), "tensor")
    down_part = lax.dot_general(
        block_input, mix_term, contract_rows, preferred_element_type=jnp.float32
    )
    up_part = lax.dot_general(
        narrow_product, value_gradient, contract_rows, preferred_element_type=jnp.float32
    )
    down_total, up_total = (
        lax.psum_scatter(
            down_part.astype(jnp.bfloat16), "dp", scatter_dimension=0, tiled=True
        ).astype(jnp.float32),
        lax.psum_scatter(
            up_part.astype(jnp.bfloat16), "dp", scatter_dimension=0, tiled=True
        ).astype(jnp.float32),
    )
    token_factor = (token_rows * lax.axis_size("section") * lax.axis_size("dp")) ** (-0.5)
    adapter_factor = (token_rows * lax.axis_size("dp")) ** (-0.5)
    grad_out = summed[:, :local_width] * token_factor
    grad_value_proj = summed[:, local_width:] * token_factor
    return (
        grad_out,
        grad_value_proj,
        grad_query,
        grad_key,
        (down_total * adapter_factor)[None],
        (up_total * adapter_factor)[None],
    )


def solution(mesh):
    return jax.shard_map(
        local,
        mesh=mesh,
        in_specs=(
            P(("section", "dp"), None),
            P(("section", "dp"), None),
            P(("section", "dp"), "tensor"),
            P(("section", "dp"), "tensor"),
            P(("section", "dp"), "tensor"),
            P(("section", "dp")),
            P(("section", "dp"), "tensor"),
            P("section", None, None),
            P("section", None, "tensor"),
        ),
        out_specs=(
            P(("section", "dp"), "tensor"),
            P(("section", "dp"), "tensor"),
            P(("section", "dp"), "tensor"),
            P(("section", "dp"), "tensor"),
            P("section", "dp", None),
            P("section", "dp", "tensor"),
        ),
        check_vma=False,
    )
```

profile of v0, /device:TPU:0, one launch (start us, length us, event | category | flops | bytes accessed | tf_op | source)
XLA Modules:
  0.0 589.8 jit_solution(15455212225179713954)
XLA Ops:
  7.2 0.7 all-gather.2.cloned.1.call-update
  8.0 2.3 copy.32
  10.3 1.4 copy.33
  11.7 1.7 copy.36
  13.4 1.0 fusion.41
  14.3 6.2 %fusion.51 = (f32[6,512]{1,0:T(8,128)S(1)}, f32[6,512,512]{1,2,0:T(8,128)}) fusion(pred[512,512]{0,1:T(8,128)(4,1)S(1)} %fusion.41, bf16[512,6,128]{0,2,1:T(8,128)(2,1)} %bitcast.63, bf16[512,6,128]{0,2,1:T(8,128)(2,1)S(1)} %bitcast.61), kind=kOutput, calls=%fused_computation.49 | convolution fusion | flops 408945152 | bytes 8138752 | tf_op jit(solution)/shard_map/sub | solution.py:27
  20.5 4.9 fusion.24
  25.5 125.5 %all-gather.2.cloned.1.call-done = bf16[6144,768]{1,0:T(8,128)(2,1)} async-done(((bf16[768,768]{1,0:T(8,128)(2,1)}), bf16[6144,768]{1,0:T(8,128)(2,1)}) %all-gather.2.cloned.1.call-update) | async-done | bytes 9437200 | tf_op jit(solution)/shard_map/all_gather | solution.py:73
  150.9 10.6 %convolution_convert_fusion.3 = bf16[512,768]{1,0:T(8,128)(2,1)} fusion(bf16[512,6144]{1,0:T(8,128)(2,1)} %param.10, bf16[6144,768]{1,0:T(8,128)(2,1)} %all-gather.2.cloned.1.call-done), kind=kOutput, calls=%fused_computation.33 | convolution fusion | flops 4832231424 | bytes 16515072 | tf_op jit(solution)/shard_map/dot_general | solution.py:71
  161.5 1.4 copy.38
  162.9 4.0 fusion.27
  166.9 0.9 copy-done.5
  167.8 1.1 convolution_convert_fusion.5
  169.0 6.1 %convolution_convert_fusion.4 = bf16[128,768]{1,0:T(8,128)(2,1)} fusion(bf16[512,768]{0,1:T(8,128)(2,1)} %bitcast.68, bf16[512,6144]{1,0:T(8,128)(2,1)} %param.9, bf16[1,6144,128]{2,1,0:T(8,128)(2,1)S(1)} %copy-done), kind=kOutput, calls=%fused_computation.34 | convolution fusion | flops 906133504 | bytes 8847360 | tf_op jit(solution)/shard_map/dot_general | solution.py:103
  175.1 23.5 %all-reduce.2.cloned.1.call-done = bf16[512,128]{1,0:T(8,128)(2,1)} async-done(((bf16[512,128]{1,0:T(8,128)(2,1)}), bf16[512,128]{1,0:T(8,128)(2,1)}) %all-reduce.2.cloned.1.call-update) | async-done | bytes 131088 | tf_op jit(solution)/shard_map/psum | solution.py:99
  198.6 5.0 fusion.4
  203.9 8.1 %fusion.2 = bf16[6144,768]{0,1:T(8,128)(2,1)S(1)} fusion(bf16[512,768]{0,1:T(8,128)(2,1)S(1)} %bitcast.70, bf16[512,6144]{1,0:T(8,128)(2,1)} %param.10), kind=kOutput, calls=%fused_computation.5 | convolution fusion | flops 4836556800 | bytes 16515072 | tf_op jit(solution)/shard_map/dot_general | solution.py:80
  212.1 8.1 %fusion.3 = bf16[6144,768]{0,1:T(8,128)(2,1)S(1)} fusion(bf16[512,768]{0,1:T(8,128)(2,1)S(1)} %bitcast.69, bf16[512,6144]{1,0:T(8,128)(2,1)} %param.9), kind=kOutput, calls=%fused_computation.6 | convolution fusion | flops 4836556800 | bytes 16515072 | tf_op jit(solution)/shard_map/dot_general | solution.py:81
  220.2 21.3 %pad_maximum_fusion = bf16[6144,1536]{0,1:T(8,128)(2,1)} fusion(bf16[6144,768]{0,1:T(8,128)(2,1)S(1)} %fusion.3, bf16[6144,768]{0,1:T(8,128)(2,1)S(1)} %fusion.2), kind=kLoop, calls=%fused_computation.2 | loop fusion | flops 37748736 | bytes 37748736 | tf_op jit(solution)/shard_map/concatenate | solution.py:85
  241.5 3.7 fusion.52
  245.2 9.9 %fusion.33 = bf16[6,512,128]{1,2,0:T(8,128)(2,1)S(1)} fusion(bf16[512,6,128]{0,2,1:T(8,128)(2,1)S(1)} %bitcast.64, f32[6,512,512]{1,2,0:T(8,128)} %fusion.52, f32[6,512,512]{1,2,0:T(8,128)} %get-tuple-element.21, f32[6,512]{1,0:T(8,128)S(1)} %get-tuple-element.20), kind=kOutput, calls=%fused_computation.32 | convolution fusion | flops 414060032 | bytes 14168064 | tf_op jit(solution)/shard_map/hqk,qhd->khd/dot_general | solution.py:44
  255.1 1.2 copy.47
  256.3 10.9 %fusion.30 = bf16[6,512,128]{1,2,0:T(8,128)(2,1)S(1)} fusion(bf16[512,6,128]{0,2,1:T(8,128)(2,1)S(1)} %bitcast.62, f32[6,512,512]{1,2,0:T(8,128)} %fusion.52, f32[6,512,512]{1,2,0:T(8,128)} %get-tuple-element.21, f32[6,512]{1,0:T(8,128)S(1)} %get-tuple-element.20), kind=kOutput, calls=%fused_computation.31 | convolution fusion | flops 414060032 | bytes 14168064 | tf_op jit(solution)/shard_map/hqk,khd->qhd/dot_general | solution.py:41
  267.2 1.2 copy.46
  268.4 1.4 multiply_bitcast_fusion.1
  269.8 1.1 multiply_bitcast_fusion
  270.9 1.1 copy.48
  272.1 300.6 %reduce-scatter.4.cloned.1.call-done = bf16[768,1536]{0,1:T(8,128)(2,1)} async-done(((bf16[6144,1536]{0,1:T(8,128)(2,1)}), bf16[768,1536]{0,1:T(8,128)(2,1)}) %reduce-scatter.4.cloned.1.call-update) | async-done | bytes 2359312 | tf_op jit(solution)/shard_map/reduce_scatter | solution.py:84
  572.7 2.0 convert_element_type.64
  574.7 2.5 slice_multiply_fusion
  577.2 3.0 copy.45
  580.3 3.0 copy.44
  (28 shorter events, 0.5 us)
Async XLA Ops:
  7.2 161.8 %copy-start = (bf16[1,6144,128]{2,1,0:T(8,128)(2,1)S(1)}, bf16[1,6144,128]{2,1,0:T(8,128)(2,1)}, u32[]{:S(2)}) copy-start(bf16[1,6144,128]{2,1,0:T(8,128)(2,1)} %param.16) | copy-start | bytes 4718596
  7.2 143.7 %all-gather.2.cloned.1.call-start = ((), (), s32[]{:S(2)}) async-start(), calls=%async_computation.3 | async-start | bytes 10616832 | tf_op jit(solution)/shard_map/all_gather | solution.py:73
  7.9 190.7 %all-reduce.2.cloned.1.call-start = ((), (), s32[]{:S(2)}) async-start(), calls=%async_computation.5 | async-start | bytes 262144 | tf_op jit(solution)/shard_map/psum | solution.py:99
  11.7 8.8 %copy-start.2 = (bf16[512,768]{0,1:T(8,128)(2,1)}, bf16[512,768]{0,1:T(8,128)(2,1)S(1)}, u32[]{:S(2)}) copy-start(bf16[512,768]{0,1:T(8,128)(2,1)S(1)} %copy.33) | copy-start | bytes 2359300
  162.9 4.9 copy-start.7
  166.9 0.9 copy-start.5
  168.9 99.5 %reduce-scatter.8.cloned.1.call-start = ((), (), s32[]{:S(2)}) async-start(), calls=%async_computation.7 | async-start | bytes 245760 | tf_op jit(solution)/shard_map/reduce_scatter | solution.py:110
  175.1 28.8 %copy-start.8 = (bf16[6,512,128]{1,2,0:T(8,128)(2,1)S(1)}, bf16[6,512,128]{1,2,0:T(8,128)(2,1)}, u32[]{:S(2)}) copy-start(bf16[6,512,128]{1,2,0:T(8,128)(2,1)} %fusion.24) | copy-start | bytes 2359300
  175.1 94.8 %reduce-scatter.6.cloned.1.call-start = ((), (), s32[]{:S(2)}) async-start(), calls=%async_computation.6 | async-start | bytes 1966080 | tf_op jit(solution)/shard_map/reduce_scatter | solution.py:107
  203.7 369.0 %reduce-scatter.4.cloned.1.call-start = ((), (), s32[]{:S(2)}) async-start(), calls=%async_computation.4 | async-start | bytes 21233664 | tf_op jit(solution)/shard_map/reduce_scatter | solution.py:84
  203.9 8.1 %copy-start.6 = (bf16[6,128,512]{2,1,0:T(8,128)(2,1)S(1)}, bf16[6,128,512]{2,1,0:T(8,128)(2,1)}, u32[]{:S(2)}) copy-start(bf16[6,128,512]{2,1,0:T(8,128)(2,1)} %copy-done.5) | copy-start | bytes 2359300
  241.5 3.7 copy-start.4
  245.2 11.1 %copy-start.3 = (bf16[512,768]{0,1:T(8,128)(2,1)S(1)}, bf16[512,768]{0,1:T(8,128)(2,1)}, u32[]{:S(2)}) copy-start(bf16[512,768]{0,1:T(8,128)(2,1)} %copy-done.2) | copy-start | bytes 2359300
  574.7 8.6 %copy-start.1 = (bf16[1,6144,128]{2,1,0:T(8,128)(2,1)S(1)}, bf16[1,6144,128]{2,1,0:T(8,128)(2,1)}, u32[]{:S(2)}) copy-start(bf16[1,6144,128]{2,1,0:T(8,128)(2,1)} %param.16) | copy-start | bytes 4718596
Sparse Core Ops, SparseCore 0:
  10.1 140.7 all-gather.1
  169.0 29.5 all-reduce.1
  201.0 19.3 reduce-scatter.7
  223.1 33.4 reduce-scatter.5
  260.3 312.2 reduce-scatter.3
where the time goes:
time: 590 us
  waiting for transfers between devices  450 us (76%)
  matrix products  78.6 us (13%)
  other arithmetic  29.3 us (5%)
  local copies, waits for them, and re-layouts  17.3 us (3%)
  between operations  13.9 us (2%)
    reduce_scatter x1, waiting for transfers between devices, local(): lax.psum_scatter(jnp.concatenate([out_term, value_term], axis=1).astype(j...  301 us
    all_gather x1, waiting for transfers between devices, local(): lax.all_gather(output_weight, ('section', 'dp'), axis=0, tiled=True)  125 us
    psum x1, waiting for transfers between devices, local(): mix_term = lax.psum(mix_part.astype(jnp.bfloat16), 'tensor')  23.5 us
    concatenate x1, other arithmetic, local(): jnp.concatenate([out_term, value_term], axis=1).astype(jnp.bfloat16)  21.3 us
    unnamed x26, local copies, waits for them, and re-layouts  15.9 us
  transfers between devices with their start and end apart: 5, of which 3 were waited for; matrix products, arithmetic and copies ran while one was open for 16% of the time, Pallas kernels for 0%

commit v1 on v0

--- a/solution.py
+++ b/solution.py
@@ -96,7 +96,7 @@
         (((1,), (1,)), ((), ())),
         preferred_element_type=jnp.float32,
     )
-    mix_term = lax.psum(mix_part.astype(jnp.bfloat16), "tensor")
+    mix_term = jnp.sum(lax.all_gather(mix_part.astype(jnp.bfloat16), "tensor"), axis=0)
     down_part = lax.dot_general(
         block_input, mix_term, contract_rows, preferred_element_type=jnp.float32
     )

time: 590 us -> 563 us (0.954)
  waiting for transfers between devices: 450 us -> 416 us
  blocking collectives: 0 us -> 7.17 us
    psum x1 -> x0, waiting for transfers between devices: 23.5 us -> none  [local(): mix_term = lax.psum(mix_part.astype(jnp.bfloat16), 'tensor')]
    reduce_scatter x1, waiting for transfers between devices: 301 us -> 290 us  [local(): lax.psum_scatter(jnp.concatenate([out_term, value_term], axis=1).astype(j...]
    all_gather x0 -> x1, blocking collectives: none -> 7.17 us  [local(): lax.all_gather(mix_part.astype(jnp.bfloat16), 'tensor')]
  transfers between devices with their start and end apart: 5 -> 4, of which waited for: 3 -> 2; matrix products, arithmetic and copies ran while one was open for 16% -> 16% of each run, Pallas kernels for 0% -> 0%
where the time goes in v1:
time: 563 us; the launch traced here: 562 us
  waiting for transfers between devices  416 us (74%)
  matrix products  77.9 us (14%)
  other arithmetic  29.3 us (5%)
  local copies, waits for them, and re-layouts  17.3 us (3%)
  between operations  13.9 us (2%)
  blocking collectives  7.17 us (1%)
    reduce_scatter x1, waiting for transfers between devices, local(): lax.psum_scatter(jnp.concatenate([out_term, value_term], axis=1).astype(j...  290 us
    all_gather x1, waiting for transfers between devices, local(): lax.all_gather(output_weight, ('section', 'dp'), axis=0, tiled=True)  125 us
    concatenate x1, other arithmetic, local(): jnp.concatenate([out_term, value_term], axis=1).astype(jnp.bfloat16)  21.2 us
    unnamed x26, local copies, waits for them, and re-layouts  15.9 us
  transfers between devices with their start and end apart: 4, of which 2 were waited for; matrix products, arithmetic and copies ran while one was open for 16% of the time, Pallas kernels for 0%

profile of v1, /device:TPU:0, one launch (start us, length us, event | category | flops | bytes accessed | tf_op | source)
XLA Modules:
  0.0 562.2 jit_solution(18219163821233922454)
XLA Ops:
  7.2 0.7 all-gather.3.cloned.1.call-update
  8.0 2.3 copy.32
  10.3 1.4 copy.33
  11.7 1.7 copy.36
  13.4 1.0 fusion.41
  14.3 6.2 %fusion.51 = (f32[6,512]{1,0:T(8,128)S(1)}, f32[6,512,512]{1,2,0:T(8,128)}) fusion(pred[512,512]{0,1:T(8,128)(4,1)S(1)} %fusion.41, bf16[512,6,128]{0,2,1:T(8,128)(2,1)} %bitcast.65, bf16[512,6,128]{0,2,1:T(8,128)(2,1)S(1)} %bitcast.63), kind=kOutput, calls=%fused_computation.49 | convolution fusion | flops 408945152 | bytes 8138752 | tf_op jit(solution)/shard_map/sub | solution.py:27
  20.5 4.9 fusion.24
  25.5 125.5 %all-gather.3.cloned.1.call-done = bf16[6144,768]{1,0:T(8,128)(2,1)} async-done(((bf16[768,768]{1,0:T(8,128)(2,1)}), bf16[6144,768]{1,0:T(8,128)(2,1)}) %all-gather.3.cloned.1.call-update) | async-done | bytes 9437200 | tf_op jit(solution)/shard_map/all_gather | solution.py:73
  150.9 10.6 %convolution_convert_fusion.3 = bf16[512,768]{1,0:T(8,128)(2,1)} fusion(bf16[512,6144]{1,0:T(8,128)(2,1)} %param.10, bf16[6144,768]{1,0:T(8,128)(2,1)} %all-gather.3.cloned.1.call-done), kind=kOutput, calls=%fused_computation.33 | convolution fusion | flops 4832231424 | bytes 16515072 | tf_op jit(solution)/shard_map/dot_general | solution.py:71
  161.5 1.4 copy.38
  162.9 4.0 fusion.27
  166.9 0.9 copy-done.5
  167.8 0.4 convolution_convert_fusion.5
  168.2 6.1 %convolution_convert_fusion.4 = bf16[128,768]{1,0:T(8,128)(2,1)} fusion(bf16[512,768]{0,1:T(8,128)(2,1)} %bitcast.70, bf16[512,6144]{1,0:T(8,128)(2,1)} %param.9, bf16[1,6144,128]{2,1,0:T(8,128)(2,1)S(1)} %copy-done), kind=kOutput, calls=%fused_computation.34 | convolution fusion | flops 906133504 | bytes 8847360 | tf_op jit(solution)/shard_map/dot_general | solution.py:103
  174.4 7.2 %all-gather = bf16[2048,128]{1,0:T(8,128)(2,1)S(1)} all-gather(bf16[512,128]{1,0:T(8,128)(2,1)S(1)} %convolution_convert_fusion.5), channel_id=2, replica_groups=mesh['tensor'=4,'section'=2,'dp'=4] {'tensor'}, dimensions={0}, use_global_device_ids=true | all-gather | bytes 655360 | tf_op jit(solution)/shard_map/all_gather | solution.py:99
  181.6 5.0 fusion.4
  187.0 8.1 %fusion.2 = bf16[6144,768]{0,1:T(8,128)(2,1)S(1)} fusion(bf16[512,768]{0,1:T(8,128)(2,1)S(1)} %bitcast.72, bf16[512,6144]{1,0:T(8,128)(2,1)} %param.10), kind=kOutput, calls=%fused_computation.5 | convolution fusion | flops 4836556800 | bytes 16515072 | tf_op jit(solution)/shard_map/dot_general | solution.py:80
  195.1 8.1 %fusion.3 = bf16[6144,768]{0,1:T(8,128)(2,1)S(1)} fusion(bf16[512,768]{0,1:T(8,128)(2,1)S(1)} %bitcast.71, bf16[512,6144]{1,0:T(8,128)(2,1)} %param.9), kind=kOutput, calls=%fused_computation.6 | convolution fusion | flops 4836556800 | bytes 16515072 | tf_op jit(solution)/shard_map/dot_general | solution.py:81
  203.1 21.2 %pad_maximum_fusion = bf16[6144,1536]{0,1:T(8,128)(2,1)} fusion(bf16[6144,768]{0,1:T(8,128)(2,1)S(1)} %fusion.3, bf16[6144,768]{0,1:T(8,128)(2,1)S(1)} %fusion.2), kind=kLoop, calls=%fused_computation.2 | loop fusion | flops 37748736 | bytes 37748736 | tf_op jit(solution)/shard_map/concatenate | solution.py:85
  224.4 3.7 fusion.52
  228.2 9.8 %fusion.33 = bf16[6,512,128]{1,2,0:T(8,128)(2,1)S(1)} fusion(bf16[512,6,128]{0,2,1:T(8,128)(2,1)S(1)} %bitcast.66, f32[6,512,512]{1,2,0:T(8,128)} %fusion.52, f32[6,512,512]{1,2,0:T(8,128)} %get-tuple-element.21, f32[6,512]{1,0:T(8,128)S(1)} %get-tuple-element.20), kind=kOutput, calls=%fused_computation.32 | convolution fusion | flops 414060032 | bytes 14168064 | tf_op jit(solution)/shard_map/hqk,qhd->khd/dot_general | solution.py:44
  238.0 1.2 copy.47
  239.1 11.0 %fusion.30 = bf16[6,512,128]{1,2,0:T(8,128)(2,1)S(1)} fusion(bf16[512,6,128]{0,2,1:T(8,128)(2,1)S(1)} %bitcast.64, f32[6,512,512]{1,2,0:T(8,128)} %fusion.52, f32[6,512,512]{1,2,0:T(8,128)} %get-tuple-element.21, f32[6,512]{1,0:T(8,128)S(1)} %get-tuple-element.20), kind=kOutput, calls=%fused_computation.31 | convolution fusion | flops 414060032 | bytes 14168064 | tf_op jit(solution)/shard_map/hqk,khd->qhd/dot_general | solution.py:41
  250.2 1.2 copy.46
  251.3 1.4 multiply_bitcast_fusion.1
  252.8 1.1 multiply_bitcast_fusion
  253.9 1.1 copy.48
  255.0 290.0 %reduce-scatter.4.cloned.1.call-done = bf16[768,1536]{0,1:T(8,128)(2,1)} async-done(((bf16[6144,1536]{0,1:T(8,128)(2,1)}), bf16[768,1536]{0,1:T(8,128)(2,1)}) %reduce-scatter.4.cloned.1.call-update) | async-done | bytes 2359312 | tf_op jit(solution)/shard_map/reduce_scatter | solution.py:84
  545.1 2.0 convert_element_type.66
  547.1 2.5 slice_multiply_fusion
  549.6 3.0 copy.45
  552.6 3.0 copy.44
  (27 shorter events, 0.5 us)
Async XLA Ops:
  7.2 161.1 %copy-start = (bf16[1,6144,128]{2,1,0:T(8,128)(2,1)S(1)}, bf16[1,6144,128]{2,1,0:T(8,128)(2,1)}, u32[]{:S(2)}) copy-start(bf16[1,6144,128]{2,1,0:T(8,128)(2,1)} %param.16) | copy-start | bytes 4718596
  7.2 143.7 %all-gather.3.cloned.1.call-start = ((), (), s32[]{:S(2)}) async-start(), calls=%async_computation.3 | async-start | bytes 10616832 | tf_op jit(solution)/shard_map/all_gather | solution.py:73
  7.9 243.4 %reduce-scatter.8.cloned.1.call-start = ((), (), s32[]{:S(2)}) async-start(), calls=%async_computation.6 | async-start | bytes 245760 | tf_op jit(solution)/shard_map/reduce_scatter | solution.py:110
  11.7 8.8 %copy-start.2 = (bf16[512,768]{0,1:T(8,128)(2,1)}, bf16[512,768]{0,1:T(8,128)(2,1)S(1)}, u32[]{:S(2)}) copy-start(bf16[512,768]{0,1:T(8,128)(2,1)S(1)} %copy.33) | copy-start | bytes 2359300
  162.9 4.9 copy-start.7
  166.9 0.9 copy-start.5
  174.3 78.4 %reduce-scatter.6.cloned.1.call-start = ((), (), s32[]{:S(2)}) async-start(), calls=%async_computation.5 | async-start | bytes 1966080 | tf_op jit(solution)/shard_map/reduce_scatter | solution.py:107
  181.6 5.3 copy-start.8
  186.7 358.4 %reduce-scatter.4.cloned.1.call-start = ((), (), s32[]{:S(2)}) async-start(), calls=%async_computation.4 | async-start | bytes 21233664 | tf_op jit(solution)/shard_map/reduce_scatter | solution.py:84
  186.9 8.1 %copy-start.6 = (bf16[6,128,512]{2,1,0:T(8,128)(2,1)S(1)}, bf16[6,128,512]{2,1,0:T(8,128)(2,1)}, u32[]{:S(2)}) copy-start(bf16[6,128,512]{2,1,0:T(8,128)(2,1)} %copy-done.5) | copy-start | bytes 2359300
  224.4 3.8 copy-start.4
  228.2 11.0 %copy-start.3 = (bf16[512,768]{0,1:T(8,128)(2,1)S(1)}, bf16[512,768]{0,1:T(8,128)(2,1)}, u32[]{:S(2)}) copy-start(bf16[512,768]{0,1:T(8,128)(2,1)} %copy-done.2) | copy-start | bytes 2359300
  547.1 8.6 %copy-start.1 = (bf16[1,6144,128]{2,1,0:T(8,128)(2,1)S(1)}, bf16[1,6144,128]{2,1,0:T(8,128)(2,1)}, u32[]{:S(2)}) copy-start(bf16[1,6144,128]{2,1,0:T(8,128)(2,1)} %param.16) | copy-start | bytes 4718596
Sparse Core Ops, SparseCore 0:
  10.1 140.7 all-gather.2
  174.5 17.5 reduce-scatter.7
  195.1 33.4 reduce-scatter.5
  232.8 312.2 reduce-scatter.3
